TPU v7x, 1024 devices: a whole 4x4x32 slice. The times are simulated.
1024 devices in a mesh: dp: 2 (over x_hi), outer: 128 (over z, x_lo, core), inner: 4 (over y).
Axes of the slice: x: 4 (x_hi: 2, x_lo: 2; x = x_hi * 2 + x_lo), y: 4, z: 32, core: 2. Of those that a mesh axis runs over, the one named last changes fastest.
Arguments:
- queries: bfloat16 [65536, 4096], P(('outer', 'inner'), 'dp'), may hold values from -512 to 512
- out_grad: bfloat16 [65536, 4096], P(('outer', 'inner'), 'dp'), may hold values from -6 to 6
- key_rows: bfloat16 [65536, 512], P(('outer', 'inner')), may hold values from -14 to 14
- value_rows: bfloat16 [65536, 512], P(('outer', 'inner')), may hold values from -6 to 6
- block_order: int32 [512], replicated, may hold values from 0 to 511, each once
- block_flags: int32 [512, 5], replicated, may hold values 0 or 1
Outputs:
- query_grad: bfloat16 [65536, 4096], P(('outer', 'inner'), 'dp')
- key_grad: float32 [65536, 512], P(('outer', 'inner'), 'dp')
- value_grad: float32 [65536, 512], P(('outer', 'inner'), 'dp')
Inputs may be any that keep to these rules, and one draw needn't show every extreme that they name: `block_order`: each number appears once.
All inputs are finite; a program needn't handle non-finite values.
Results may differ from a plain program's by a relative error of at most 0.005.
Values may be sent and summed in bfloat16 or wider, within the bound.
No kernel may reach another device: no remote copies, remote signals or barrier semaphores. Data moves between devices by JAX's collectives and lax.ppermute only.
A program may use at most 32 MiB of HBM per device.

v0:
```python
import math

import jax
import jax.numpy as jnp
from jax import lax
from jax.sharding import PartitionSpec as P

HD = 128


def passed_along(x, axis, by):
    devices = lax.axis_size(axis)
    return lax.ppermute(x, axis, [(i, (i + by) % devices) for i in range(devices)])


def arrange(partial_value, returned, inner_size, member_index, row_count, key_heads, split_count):
    blocks = partial_value.reshape(inner_size, row_count, key_heads, HD)
    own_slot = (jnp.arange(inner_size, dtype=jnp.int32) == member_index)[:, None, None, None]
    blocks = blocks + jnp.where(own_slot, returned[None], 0.0)
    blocks = blocks.reshape(
        inner_size, row_count, split_count, key_heads // split_count, HD
    ).transpose(2, 0, 1, 3, 4)
    return blocks.reshape(split_count * inner_size * row_count, key_heads // split_count, HD)


def body(queries, out_grad, key_rows, value_rows, block_order, block_flags):
    row_count = queries.shape[0]
    key_heads = key_rows.shape[1] // HD
    local_groups = queries.shape[1] // (key_heads * HD)
    inner_size = lax.axis_size("inner")
    outer_size = lax.axis_size("outer")
    split_count = lax.axis_size("dp")
    outer_index = lax.axis_index("outer")
    member_index = lax.axis_index("inner")
    shard_index = outer_index * inner_size + member_index
    previous = (outer_index + outer_size - 1) % outer_size * inner_size + member_index
    group_keys, group_values = (
        lax.all_gather(key_rows, "inner", axis=0, tiled=True),
        lax.all_gather(value_rows, "inner", axis=0, tiled=True),
    )
    prev_keys, prev_values = passed_along((key_rows, value_rows), "outer", 1)
    group_span = inner_size * row_count
    key_window = jnp.concatenate([group_keys, prev_keys], 0).reshape(
        group_span + row_count, key_heads, HD
    )
    value_window = jnp.concatenate([group_values, prev_values], 0).reshape(
        group_span + row_count, key_heads, HD
    )
    row_index = jnp.arange(row_count, dtype=jnp.int32)
    group_blocks = lax.dynamic_slice_in_dim(block_order, outer_index * inner_size, inner_size, 0)
    prev_block = lax.dynamic_slice_in_dim(block_order, previous, 1, 0)
    own_block = lax.dynamic_slice_in_dim(block_order, shard_index, 1, 0)
    key_pos = (
        jnp.concatenate([group_blocks, prev_block], 0)[:, None] * row_count + row_index[None, :]
    ).reshape(-1)
    query_pos = own_block * row_count + row_index
    flag_row = lax.dynamic_slice(block_flags, (shard_index, 0), (1, inner_size + 1))[0]
    allowed = (flag_row == 1) | (jnp.arange(inner_size + 1, dtype=jnp.int32) == member_index)
    visible = (key_pos[None, :] <= query_pos[:, None]) & jnp.repeat(allowed, row_count)[None, :]
    seen = visible[None]
    score_scale = 1.0 / math.sqrt(HD)
    query_stack = queries.reshape(row_count, local_groups, key_heads, HD).transpose(1, 0, 2, 3)
    grad_stack = out_grad.reshape(row_count, local_groups, key_heads, HD).transpose(1, 0, 2, 3)

    def head_group(totals, blocks_in):
        key_sum, value_sum = totals
        query_block, grad_block = blocks_in
        scores = (
            jnp.einsum("rjd,wjd->jrw", query_block, key_window, preferred_element_type=jnp.float32)
            * score_scale
        )
        row_max = jnp.max(jnp.where(seen, scores, -jnp.inf), axis=-1, keepdims=True)
        exp_scores = jnp.where(seen, jnp.exp(scores - row_max), 0.0)
        soft_weights = exp_scores / jnp.sum(exp_scores, axis=-1, keepdims=True)
        soft_low = soft_weights.astype(jnp.bfloat16)
        weight_grads = jnp.einsum(
            "rjd,wjd->jrw", grad_block, value_window, preferred_element_type=jnp.float32
        )
        row_delta = jnp.sum(soft_weights * weight_grads, axis=-1, keepdims=True)
        score_grads = (soft_weights * (weight_grads - row_delta) * score_scale).astype(jnp.bfloat16)
        query_part = jnp.einsum(
            "jrw,wjd->rjd", score_grads, key_window, preferred_element_type=jnp.float32
        ).astype(jnp.bfloat16)
        key_sum = key_sum + jnp.einsum(
            "jrw,rjd->wjd", score_grads, query_block, preferred_element_type=jnp.float32
        )
        value_sum = value_sum + jnp.einsum(
            "jrw,rjd->wjd", soft_low, grad_block, preferred_element_type=jnp.float32
        )
        return ((key_sum, value_sum), query_part)

    zero_sums = jnp.zeros((group_span + row_count, key_heads, HD), jnp.float32)
    (key_sum, value_sum), query_parts = lax.scan(
        head_group, (zero_sums, zero_sums), (query_stack, grad_stack)
    )
    query_grad = query_parts.transpose(1, 0, 2, 3).reshape(row_count, local_groups * key_heads * HD)
    back_keys, back_values = (
        passed_along(key_sum[group_span:].astype(jnp.bfloat16), "outer", -1).astype(jnp.float32),
        passed_along(value_sum[group_span:].astype(jnp.bfloat16), "outer", -1).astype(jnp.float32),
    )
    key_grad, value_grad = (
        lax.psum_scatter(
            arrange(
                key_sum[:group_span],
                back_keys,
                inner_size,
                member_index,
                row_count,
                key_heads,
                split_count,
            ),
            ("dp", "inner"),
            scatter_dimension=0,
            tiled=True,
        ),
        lax.psum_scatter(
            arrange(
                value_sum[:group_span],
                back_values,
                inner_size,
                member_index,
                row_count,
                key_heads,
                split_count,
            ),
            ("dp", "inner"),
            scatter_dimension=0,
            tiled=True,
        ),
    )
    return (query_grad, key_grad.reshape(row_count, -1), value_grad.reshape(row_count, -1))


def solution(mesh):
    placed = (
        P(("outer", "inner"), "dp"),
        P(("outer", "inner"), "dp"),
        P(("outer", "inner"), None),
        P(("outer", "inner"), None),
        P(),
        P(),
    )
    return jax.shard_map(
        body,
        mesh=mesh,
        in_specs=placed,
        out_specs=(
            P(("outer", "inner"), "dp"),
            P(("outer", "inner"), "dp"),
            P(("outer", "inner"), "dp"),
        ),
        check_vma=False,
    )
```

profile of v0, /device:TPU:32, one launch (start us, length us, event | category | flops | bytes accessed | tf_op | source)
XLA Modules:
  0.0 270.3 jit_solution(3135711149593090973)
XLA Ops:
  8.3 2.1 collective-permute-start
  11.4 3.5 %collective-permute-start.1 = (bf16[128,512]{0,1:T(8,128)(2,1)S(1)}, bf16[128,512]{0,1:T(8,128)(2,1)S(1)}, u32[]{:S(2)}, u32[]{:S(2)}) collective-permute-start(bf16[128,512]{0,1:T(8,128)(2,1)S(1)} %copy.35), channel_id=1, source_target_pairs={{0,4},{4,8},{8,12},{12,16},{16,20},{20,24},{24,28},{28,32},{32,36}... | collective-permute-start | bytes 393224 | tf_op jit(solution)/shard_map/ppermute | solution.py:13
  14.9 14.7 %all_gather.6 = bf16[512,512]{0,1:T(8,128)(2,1)S(1)} all-gather(bf16[128,512]{0,1:T(8,128)(2,1)S(1)} %copy.32), channel_id=1, replica_groups=mesh['dp'=2,'outer'=128,'inner'=4] {'inner'}, dimensions={0}, use_global_device_ids=true | all-gather | bytes 655360 | tf_op jit(solution)/shard_map/all_gather | solution.py:38
  30.4 1.3 fusion.58
  33.5 12.5 %all_gather.7 = bf16[512,512]{0,1:T(8,128)(2,1)S(1)} all-gather(bf16[128,512]{0,1:T(8,128)(2,1)S(1)} %copy.35), channel_id=1, replica_groups=mesh['dp'=2,'outer'=128,'inner'=4] {'inner'}, dimensions={0}, use_global_device_ids=true | all-gather | bytes 655360 | tf_op jit(solution)/shard_map/all_gather | solution.py:39
  50.3 59.4 %while.15 = (s32[]{:T(128)}, f32[640,4,128]{0,2,1:T(8,128)}, f32[640,4,128]{0,2,1:T(8,128)}, bf16[4,128,4,128]{3,1,2,0:T(8,128)(2,1)}, bf16[4,128,4,128]{1,3,2,0...) while((s32[]{:T(128)}, f32[640,4,128]{0,2,1:T(8,128)}, ...), condition=%wide.region_4.5_spmd.clone, body=%wide.region_0.4_spmd.clone.sunk | while | flops 427854720 | bytes 27707684 | solution.py:93
  54.1 3.2 %fusion.91 = bf16[4,128,4,128]{3,1,2,0:T(8,128)(2,1)} fusion(bf16[4,128,4,128]{3,1,2,0:T(8,128)(2,1)} %get-tuple-element.237, s32[]{:T(128)} %get-tuple-element.234, bf16[640,4,128]{2,0,1:T(8,128)(2,1)S(1)} %get-tuple-element.252, f32[4,128,640]{2,1,0:T(8,128)S(1)} %fusion.87, f32[4,128,640]{2,1,0:T(8,128)S(1)} %get-tuple-element.219, ...), kind=kOutput, calls=%fused_computation.22.clone.1 | convolution fusion | flops 86246528 | bytes 6033920 | tf_op jit(solution)/shard_map/while/body/eval_jaxpr/jrw,wjd->rjd/dot_general | solution.py:81
  57.3 2.4 fusion.90
  59.8 4.6 %fusion.89 = f32[640,4,128]{0,2,1:T(8,128)} fusion(f32[640,4,128]{0,2,1:T(8,128)} %get-tuple-element.235, f32[4,128,640]{2,1,0:T(8,128)S(1)} %fusion.87, pred[]{:T(512)S(6)} %compare.4, bf16[4,128,4,128]{1,3,2,0:T(8,128)(2,1)} %get-tuple-element.251, s32[]{:T(128)} %get-tuple-element.234, f32[4,128,640]{2,1,0:T(8,128)S(1)} %get-tuple-element.219, ...), kind=kOutput, calls=%fused_computation.15.clone.1 | convolution fusion | flops 86836352 | bytes 8000001 | tf_op jit(solution)/shard_map/while/body/eval_jaxpr/jrw,rjd->wjd/dot_general | solution.py:84
  68.2 3.2 %fusion.91 = bf16[4,128,4,128]{3,1,2,0:T(8,128)(2,1)} fusion(bf16[4,128,4,128]{3,1,2,0:T(8,128)(2,1)} %get-tuple-element.237, s32[]{:T(128)} %get-tuple-element.234, bf16[640,4,128]{2,0,1:T(8,128)(2,1)S(1)} %get-tuple-element.252, f32[4,128,640]{2,1,0:T(8,128)S(1)} %fusion.87, f32[4,128,640]{2,1,0:T(8,128)S(1)} %get-tuple-element.219, ...), kind=kOutput, calls=%fused_computation.22.clone.1 | convolution fusion | flops 86246528 | bytes 6033920 | tf_op jit(solution)/shard_map/while/body/eval_jaxpr/jrw,wjd->rjd/dot_general | solution.py:81
  71.5 2.9 %fusion.90 = f32[640,4,128]{0,2,1:T(8,128)} fusion(f32[640,4,128]{0,2,1:T(8,128)} %get-tuple-element.236, pred[]{:T(512)S(6)} %compare.4, bf16[4,128,4,128]{1,3,2,0:T(8,128)(2,1)} %get-tuple-element.253, s32[]{:T(128)} %get-tuple-element.234, f32[4,128,640]{2,1,0:T(8,128)S(1)} %get-tuple-element.219, f32[4,128]{1,0:T(4,128)S(1)} %get-tuple-element.220), kind=kOutput, calls=%fused_computation.13.clone.1 | convolution fusion | flops 85196800 | bytes 4065793 | tf_op jit(solution)/shard_map/while/body/eval_jaxpr/jrw,rjd->wjd/dot_general | solution.py:87
  74.4 5.1 %fusion.89 = f32[640,4,128]{0,2,1:T(8,128)} fusion(f32[640,4,128]{0,2,1:T(8,128)} %get-tuple-element.235, f32[4,128,640]{2,1,0:T(8,128)S(1)} %fusion.87, pred[]{:T(512)S(6)} %compare.4, bf16[4,128,4,128]{1,3,2,0:T(8,128)(2,1)} %get-tuple-element.251, s32[]{:T(128)} %get-tuple-element.234, f32[4,128,640]{2,1,0:T(8,128)S(1)} %get-tuple-element.219, ...), kind=kOutput, calls=%fused_computation.15.clone.1 | convolution fusion | flops 86836352 | bytes 8000001 | tf_op jit(solution)/shard_map/while/body/eval_jaxpr/jrw,rjd->wjd/dot_general | solution.py:84
  83.3 3.2 %fusion.91 = bf16[4,128,4,128]{3,1,2,0:T(8,128)(2,1)} fusion(bf16[4,128,4,128]{3,1,2,0:T(8,128)(2,1)} %get-tuple-element.237, s32[]{:T(128)} %get-tuple-element.234, bf16[640,4,128]{2,0,1:T(8,128)(2,1)S(1)} %get-tuple-element.252, f32[4,128,640]{2,1,0:T(8,128)S(1)} %fusion.87, f32[4,128,640]{2,1,0:T(8,128)S(1)} %get-tuple-element.219, ...), kind=kOutput, calls=%fused_computation.22.clone.1 | convolution fusion | flops 86246528 | bytes 6033920 | tf_op jit(solution)/shard_map/while/body/eval_jaxpr/jrw,wjd->rjd/dot_general | solution.py:81
  86.6 2.9 %fusion.90 = f32[640,4,128]{0,2,1:T(8,128)} fusion(f32[640,4,128]{0,2,1:T(8,128)} %get-tuple-element.236, pred[]{:T(512)S(6)} %compare.4, bf16[4,128,4,128]{1,3,2,0:T(8,128)(2,1)} %get-tuple-element.253, s32[]{:T(128)} %get-tuple-element.234, f32[4,128,640]{2,1,0:T(8,128)S(1)} %get-tuple-element.219, f32[4,128]{1,0:T(4,128)S(1)} %get-tuple-element.220), kind=kOutput, calls=%fused_computation.13.clone.1 | convolution fusion | flops 85196800 | bytes 4065793 | tf_op jit(solution)/shard_map/while/body/eval_jaxpr/jrw,rjd->wjd/dot_general | solution.py:87
  89.5 5.1 %fusion.89 = f32[640,4,128]{0,2,1:T(8,128)} fusion(f32[640,4,128]{0,2,1:T(8,128)} %get-tuple-element.235, f32[4,128,640]{2,1,0:T(8,128)S(1)} %fusion.87, pred[]{:T(512)S(6)} %compare.4, bf16[4,128,4,128]{1,3,2,0:T(8,128)(2,1)} %get-tuple-element.251, s32[]{:T(128)} %get-tuple-element.234, f32[4,128,640]{2,1,0:T(8,128)S(1)} %get-tuple-element.219, ...), kind=kOutput, calls=%fused_computation.15.clone.1 | convolution fusion | flops 86836352 | bytes 8000001 | tf_op jit(solution)/shard_map/while/body/eval_jaxpr/jrw,rjd->wjd/dot_general | solution.py:84
  98.4 3.2 %fusion.91 = bf16[4,128,4,128]{3,1,2,0:T(8,128)(2,1)} fusion(bf16[4,128,4,128]{3,1,2,0:T(8,128)(2,1)} %get-tuple-element.237, s32[]{:T(128)} %get-tuple-element.234, bf16[640,4,128]{2,0,1:T(8,128)(2,1)S(1)} %get-tuple-element.252, f32[4,128,640]{2,1,0:T(8,128)S(1)} %fusion.87, f32[4,128,640]{2,1,0:T(8,128)S(1)} %get-tuple-element.219, ...), kind=kOutput, calls=%fused_computation.22.clone.1 | convolution fusion | flops 86246528 | bytes 6033920 | tf_op jit(solution)/shard_map/while/body/eval_jaxpr/jrw,wjd->rjd/dot_general | solution.py:81
  101.7 2.9 %fusion.90 = f32[640,4,128]{0,2,1:T(8,128)} fusion(f32[640,4,128]{0,2,1:T(8,128)} %get-tuple-element.236, pred[]{:T(512)S(6)} %compare.4, bf16[4,128,4,128]{1,3,2,0:T(8,128)(2,1)} %get-tuple-element.253, s32[]{:T(128)} %get-tuple-element.234, f32[4,128,640]{2,1,0:T(8,128)S(1)} %get-tuple-element.219, f32[4,128]{1,0:T(4,128)S(1)} %get-tuple-element.220), kind=kOutput, calls=%fused_computation.13.clone.1 | convolution fusion | flops 85196800 | bytes 4065793 | tf_op jit(solution)/shard_map/while/body/eval_jaxpr/jrw,rjd->wjd/dot_general | solution.py:87
  104.6 5.1 %fusion.89 = f32[640,4,128]{0,2,1:T(8,128)} fusion(f32[640,4,128]{0,2,1:T(8,128)} %get-tuple-element.235, f32[4,128,640]{2,1,0:T(8,128)S(1)} %fusion.87, pred[]{:T(512)S(6)} %compare.4, bf16[4,128,4,128]{1,3,2,0:T(8,128)(2,1)} %get-tuple-element.251, s32[]{:T(128)} %get-tuple-element.234, f32[4,128,640]{2,1,0:T(8,128)S(1)} %get-tuple-element.219, ...), kind=kOutput, calls=%fused_computation.15.clone.1 | convolution fusion | flops 86836352 | bytes 8000001 | tf_op jit(solution)/shard_map/while/body/eval_jaxpr/jrw,rjd->wjd/dot_general | solution.py:84
  109.7 1.7 slice.23
  111.4 1.9 collective-permute-start.2
  114.3 3.8 %collective-permute-start.3 = (bf16[128,4,128]{0,2,1:T(8,128)(2,1)S(1)}, bf16[128,4,128]{0,2,1:T(8,128)(2,1)S(1)}, u32[]{:S(2)}, u32[]{:S(2)}) collective-permute-start(bf16[128,4,128]{0,2,1:T(8,128)(2,1)S(1)} %slice.22), channel_id=1, source_target_pairs={{0,508},{4,0},{8,4},{12,8},{16,12},{20,16},{24,20},{28,24},{32,28}... | collective-permute-start | bytes 393224 | tf_op jit(solution)/shard_map/ppermute | solution.py:13
  121.8 2.5 select_add_fusion
  124.3 1.3 dynamic-slice
  127.9 133.2 %all-reduce.5.cloned.1.call-done = (f32[1024,2,128]{2,1,0:T(2,128)}, f32[1024,2,128]{2,1,0:T(2,128)}) async-done(((f32[1024,2,128]{2,1,0:T(2,128)}, f32[1024,2,128]{2,1,0:T(2,128)}), (f32[1024,2,128]{2,1,0:T(2,128)}, f32[1024,2,128]{2,1,0:T(2,128)})) %all-reduce.5.cloned.1.call-update) | async-done | bytes 2097168
  (71 shorter events, 32.1 us)
Async XLA Ops:
  7.2 39.5 %copy-start.2 = (bf16[128,2048]{1,0:T(8,128)(2,1)S(1)}, bf16[128,2048]{1,0:T(8,128)(2,1)}, u32[]{:S(2)}) copy-start(bf16[128,2048]{1,0:T(8,128)(2,1)} %param.8) | copy-start | bytes 1572868
  7.2 254.0 %all-reduce.5.cloned.1.call-start = ((), (), s32[]{:S(2)}) async-start(), calls=%async_computation | async-start | bytes 4194304
  8.3 39.4 %copy-start.3 = (bf16[128,2048]{1,0:T(8,128)(2,1)S(1)}, bf16[128,2048]{1,0:T(8,128)(2,1)}, u32[]{:S(2)}) copy-start(bf16[128,2048]{1,0:T(8,128)(2,1)} %param.9) | copy-start | bytes 1572868
  8.3 40.4 %collective-permute-start = (bf16[128,512]{0,1:T(8,128)(2,1)S(1)}, bf16[128,512]{0,1:T(8,128)(2,1)S(1)}, u32[]{:S(2)}, u32[]{:S(2)}) collective-permute-start(bf16[128,512]{0,1:T(8,128)(2,1)S(1)} %copy.32), channel_id=1, source_target_pairs={{0,4},{4,8},{8,12},{12,16},{16,20},{20,24},{24,28},{28,32},{32,36}... | collective-permute-start | bytes 393224 | tf_op jit(solution)/shard_map/ppermute | solution.py:13
  11.4 37.7 %collective-permute-start.1 = (bf16[128,512]{0,1:T(8,128)(2,1)S(1)}, bf16[128,512]{0,1:T(8,128)(2,1)S(1)}, u32[]{:S(2)}, u32[]{:S(2)}) collective-permute-start(bf16[128,512]{0,1:T(8,128)(2,1)S(1)} %copy.35), channel_id=1, source_target_pairs={{0,4},{4,8},{8,12},{12,16},{16,20},{20,24},{24,28},{28,32},{32,36}... | collective-permute-start | bytes 393224 | tf_op jit(solution)/shard_map/ppermute | solution.py:13
  51.7 1.1 copy-start
  65.8 1.1 copy-start
  80.9 1.1 copy-start
  96.0 1.1 copy-start
  109.7 9.7 %copy-start.1 = (f32[640,4,128]{0,2,1:T(8,128)S(1)}, f32[640,4,128]{0,2,1:T(8,128)}, u32[]{:S(2)}) copy-start(f32[640,4,128]{0,2,1:T(8,128)} %get-tuple-element.54) | copy-start | bytes 3932164
  111.4 10.2 %collective-permute-start.2 = (bf16[128,4,128]{0,2,1:T(8,128)(2,1)}, bf16[128,4,128]{0,2,1:T(8,128)(2,1)S(1)}, u32[]{:S(2)}, u32[]{:S(2)}) collective-permute-start(bf16[128,4,128]{0,2,1:T(8,128)(2,1)} %slice.23), channel_id=1, source_target_pairs={{0,508},{4,0},{8,4},{12,8},{16,12},{20,16},{24,20},{28,24},{32,28}... | collective-permute-start | bytes 393224 | tf_op jit(solution)/shard_map/ppermute | solution.py:13
  114.3 7.4 %collective-permute-start.3 = (bf16[128,4,128]{0,2,1:T(8,128)(2,1)S(1)}, bf16[128,4,128]{0,2,1:T(8,128)(2,1)S(1)}, u32[]{:S(2)}, u32[]{:S(2)}) collective-permute-start(bf16[128,4,128]{0,2,1:T(8,128)(2,1)S(1)} %slice.22), channel_id=1, source_target_pairs={{0,508},{4,0},{8,4},{12,8},{16,12},{20,16},{24,20},{28,24},{32,28}... | collective-permute-start | bytes 393224 | tf_op jit(solution)/shard_map/ppermute | solution.py:13
  124.3 2.0 copy-start.4
Sparse Core Ops, SparseCore 0:
  124.5 136.6 all-reduce.4
where the time goes:
time: 271 us; the launch traced here: 270 us
  waiting for transfers between devices  133 us (49%)
  matrix products  54.5 us (20%)
  blocking collectives  27.2 us (10%)
  local copies, waits for them, and re-layouts  21.3 us (8%)
  between operations  15.6 us (6%)
  starting transfers between devices  11.3 us (4%)
  other arithmetic  7.04 us (3%)
    unnamed x2, waiting for transfers between devices  133 us
    dot_general x4, matrix products, head_group(): jnp.einsum('jrw,rjd->wjd', score_grads, query_block, preferred_element_ty...  19.9 us
    all_gather x1, blocking collectives, body(): lax.all_gather(key_rows, 'inner', axis=0, tiled=True)  14.7 us
    dot_general x4, matrix products, head_group(): jnp.einsum('jrw,wjd->rjd', score_grads, key_window, preferred_element_typ...  12.9 us
    all_gather x1, blocking collectives, body(): lax.all_gather(value_rows, 'inner', axis=0, tiled=True)  12.5 us
    ppermute x4, starting transfers between devices, passed_along(): lax.ppermute(x, axis, [(i, (i + by) % devices) for i in range(devices)])  11.3 us
    dot_general x4, matrix products, head_group(): jnp.einsum('jrw,rjd->wjd', soft_low, grad_block, preferred_element_type=j...  11.1 us
    unnamed x18, local copies, waits for them, and re-layouts  9.15 us
  transfers between devices with their start and end apart: 5, of which 1 were waited for; matrix products, arithmetic and copies ran while one was open for 5% of the time, Pallas kernels for 0%

commit v1 on v0

v1 whole, which is shorter than its diff:
```python
import functools
import math

import jax
import jax.numpy as jnp
from jax import lax
from jax.experimental import pallas as pl
from jax.experimental.pallas import tpu as pltpu
from jax.sharding import PartitionSpec as P


HD = 128
SCALE = 1.0 / math.sqrt(HD)
LOG2E = 1.4426950408889634
VMEM = pl.BlockSpec(memory_space=pltpu.VMEM)
SMEM = pl.BlockSpec(memory_space=pltpu.SMEM)
HBM = pl.BlockSpec(memory_space=pltpu.HBM)
BF = jnp.bfloat16
F32 = jnp.float32


def passed_along(x, axis, by):
    devices = lax.axis_size(axis)
    return lax.ppermute(x, axis, [(i, (i + by) % devices) for i in range(devices)])


def lanes(start, size):
    return pl.ds(pl.multiple_of(start, 128), size)


def stay(x):
    return pltpu.with_memory_space_constraint(x, pltpu.HBM)


def limit(mib):
    return pltpu.CompilerParams(vmem_limit_bytes=mib << 20)


def pack_kernel(dims, order_hbm, flag_hbm, q_ref, g_ref, k_ref, v_ref, send_ref, kv4_ref, kv_ref, bias_ref, order_ref, flag_ref, sems):
    groups, half, members, outers = dims
    rows = kv_ref.shape[0]
    d = lax.axis_index("dp")
    outer = lax.axis_index("outer")
    member = lax.axis_index("inner")
    wide = groups * half
    moves = [(order_hbm, order_ref), (flag_hbm, flag_ref)]
    for base, ref in ((0, k_ref), (half, v_ref)):
        source = ref.at[:, lanes(d * half, half)]
        moves.append((source, kv_ref.at[:, base : base + half]))
    for g in range(groups):
        away = g * 2 * half + (1 - d) * half
        for base, ref in ((0, q_ref), (wide, g_ref)):
            at = base + g * half
            moves.append((ref.at[:, lanes(away, half)], send_ref.at[:, at : at + half]))
    for base, ref in ((0, k_ref), (half, v_ref)):
        source = ref.at[:, lanes(d * half, half)]
        for c in range(members):
            moves.append((source, kv4_ref.at[c * rows : (c + 1) * rows, base : base + half]))
    copies = [pltpu.make_async_copy(a, b, sems.at[i]) for i, (a, b) in enumerate(moves)]
    for copy in copies:
        copy.start()
    copies[0].wait()
    copies[1].wait()
    shard = outer * members + member
    before = lax.rem(outer + outers - 1, outers) * members + member
    mine = order_ref[shard]
    key_at = lax.broadcasted_iota(jnp.int32, (rows, rows), 0)
    row_at = lax.broadcasted_iota(jnp.int32, (rows, rows), 1)
    triangle = jnp.where(key_at <= row_at, 0.0, -jnp.inf).astype(F32)
    for c in range(members + 1):
        where = outer * members + c if c < members else before
        seen = jnp.logical_and(order_ref[where] < mine, flag_ref[c, shard] == 1)
        flat = jnp.full((rows, rows), jnp.where(seen, 0.0, -jnp.inf), F32)
        if c < members:
            flat = jnp.where(member == c, triangle, flat)
        bias_ref[c * rows : (c + 1) * rows, :] = flat
    for copy in copies[2:]:
        copy.wait()


def attend(q2, g2, keys, values, keys_t, bias2):
    nt = (((1,), (1,)), ((), ()))
    scores = lax.dot_general(keys, q2, nt, preferred_element_type=F32) + bias2
    top = jnp.max(scores, axis=0, keepdims=True)
    exps = jnp.exp2((scores - top) * (SCALE * LOG2E))
    weight_grads = lax.dot_general(values, g2, nt, preferred_element_type=F32)
    inverse = 1.0 / jnp.sum(exps, axis=0, keepdims=True)
    delta = jnp.sum(exps * weight_grads, axis=0, keepdims=True) * inverse
    soft = exps * inverse
    soft_low = soft.astype(BF)
    score_grads = (soft * ((weight_grads - delta) * SCALE)).astype(BF)
    value_part = jnp.dot(soft_low, g2, preferred_element_type=F32)
    key_part = jnp.dot(score_grads, q2, preferred_element_type=F32)
    query_t = jnp.dot(keys_t, score_grads, preferred_element_type=F32)
    return query_t, key_part, value_part


def heads_kernel(local, half, groups, members, *refs):
    if local:
        q_ref, g_ref, kv_ref, prev_ref, bias_ref, dq_ref, dk_ref, dv_ref, keys, values, keys_t = refs
    else:
        (qg_ref, kv_ref, prev_ref, bias_ref, dk_in, dv_in, dq_ref, part_ref, back_ref, keys, values, keys_t, dk_ref, dv_ref) = refs
    rows = prev_ref.shape[0]
    span = members * rows
    per = half // HD
    d = lax.axis_index("dp")
    for j in range(per):
        keys[j, :span, :] = kv_ref[:, j * HD : (j + 1) * HD]
        keys[j, span:, :] = prev_ref[:, j * HD : (j + 1) * HD]
        values[j, :span, :] = kv_ref[:, half + j * HD : half + (j + 1) * HD]
        values[j, span:, :] = prev_ref[:, half + j * HD : half + (j + 1) * HD]
        keys_t[j] = keys[j].T
    pairs = groups // 2

    def step(i, carry):
        j, pair = i // pairs, i % pairs
        wide = groups * half
        if local:
            at = [(2 * pair + e) * 2 * half + d * half + j * HD for e in range(2)]
            q2 = jnp.concatenate([q_ref[:, lanes(a, HD)] for a in at], 0)
            g2 = jnp.concatenate([g_ref[:, lanes(a, HD)] for a in at], 0)
        else:
            at = [(2 * pair + e) * half + j * HD for e in range(2)]
            q2 = jnp.concatenate([qg_ref[:, lanes(a, HD)] for a in at], 0)
            g2 = jnp.concatenate([qg_ref[:, lanes(wide + a, HD)] for a in at], 0)
        bias = bias_ref[...]
        query_t, key_part, value_part = attend(
            q2, g2, keys[j], values[j], keys_t[j], jnp.concatenate([bias, bias], 1)
        )
        for e in range(2):
            out_at = (2 * pair + e) * half + j * HD
            dq_ref[:, lanes(out_at, HD)] = query_t[:, e * rows : (e + 1) * rows].T.astype(BF)
        if local:
            first = pair == 0

            @pl.when(first)
            def _():
                dk_ref[j] = key_part
                dv_ref[j] = value_part

            @pl.when(jnp.logical_not(first))
            def _():
                dk_ref[j] += key_part
                dv_ref[j] += value_part
        else:
            first = pair == 0

            @pl.when(first)
            def _():
                dk_ref[j] = dk_in[j] + key_part
                dv_ref[j] = dv_in[j] + value_part

            @pl.when(jnp.logical_not(first))
            def _():
                dk_ref[j] += key_part
                dv_ref[j] += value_part

        return carry

    lax.fori_loop(0, per * pairs, step, 0)
    if not local:
        for j in range(per):
            for ref, base in ((dk_ref, 0), (dv_ref, half)):
                at = base + j * HD
                part_ref[:, at : at + HD] = ref[j, :span, :].astype(BF)
                back_ref[:, at : at + HD] = ref[j, span:, :].astype(BF)


def finish_kernel(half, groups, members, part_ref, back_ref, own_dq_ref, far_dq_ref, dq_ref, dk_ref, dv_ref):
    rows = back_ref.shape[0]
    d = lax.axis_index("dp")
    for g in range(groups):
        dq_ref[:, lanes(g * 2 * half + d * half, half)] = own_dq_ref[:, g * half : (g + 1) * half]
        dq_ref[:, lanes(g * 2 * half + (1 - d) * half, half)] = far_dq_ref[:, g * half : (g + 1) * half]
    total = back_ref[...].astype(F32)
    for c in range(members):
        total = total + part_ref[c * rows : (c + 1) * rows, :].astype(F32)
    dk_ref[...] = total[:, :half]
    dv_ref[...] = total[:, half:]


def step(queries, out_grad, key_rows, value_rows, block_order, block_flags):
    rows = queries.shape[0]
    key_heads = key_rows.shape[1] // HD
    groups = queries.shape[1] // (key_heads * HD)
    members = lax.axis_size("inner")
    outers = lax.axis_size("outer")
    half = key_heads * HD // lax.axis_size("dp")
    per = half // HD
    window = (members + 1) * rows
    S = jax.ShapeDtypeStruct
    send, kv4, kv, bias = pl.pallas_call(
        functools.partial(pack_kernel, (groups, half, members, outers)),
        out_shape=(
            S((rows, 2 * groups * half), BF),
            S((members * rows, 2 * half), BF),
            S((rows, 2 * half), BF),
            S((window, rows), F32),
        ),
        in_specs=[HBM] * 6,
        out_specs=(VMEM,) * 4,
        scratch_shapes=[
            pltpu.SMEM(block_order.shape, jnp.int32),
            pltpu.SMEM(block_flags.shape[::-1], jnp.int32),
            pltpu.SemaphoreType.DMA((4 + 2 * groups + 2 * members,)),
        ],
        compiler_params=limit(8),
        name="pack",
    )(*[stay(a) for a in (block_order, block_flags.T, queries, out_grad, key_rows, value_rows)])
    prev_kv = passed_along(kv, "outer", 1)
    received = passed_along(send, "dp", 1)
    group_kv = lax.all_to_all(kv4, "inner", 0, 0, tiled=True)
    scratch = [pltpu.VMEM((per, window, HD), BF), pltpu.VMEM((per, window, HD), BF), pltpu.VMEM((per, HD, window), BF)]
    cost = pl.CostEstimate(
        flops=10 * rows * window * HD * groups * per,
        transcendentals=rows * window * groups * per,
        bytes_accessed=4 * rows * window * per * groups,
    )
    own_dq, dk, dv = pl.pallas_call(
        functools.partial(heads_kernel, True, half, groups, members),
        out_shape=(S((rows, groups * half), BF), S((per, window, HD), F32), S((per, window, HD), F32)),
        in_specs=[VMEM] * 5,
        out_specs=(VMEM,) * 3,
        scratch_shapes=scratch,
        cost_estimate=cost,
        compiler_params=limit(24),
        name="own_heads",
    )(queries, out_grad, group_kv, prev_kv, bias)
    far_dq, part, back = pl.pallas_call(
        functools.partial(heads_kernel, False, half, groups, members),
        out_shape=(S((rows, groups * half), BF), S((members * rows, 2 * half), BF), S((rows, 2 * half), BF)),
        in_specs=[VMEM] * 6,
        out_specs=(VMEM,) * 3,
        scratch_shapes=scratch + [pltpu.VMEM((per, window, HD), F32), pltpu.VMEM((per, window, HD), F32)],
        cost_estimate=cost,
        compiler_params=limit(24),
        name="far_heads",
    )(received, group_kv, prev_kv, bias, dk, dv)
    far_dq = passed_along(far_dq, "dp", 1)
    part = lax.all_to_all(part, "inner", 0, 0, tiled=True)
    back = passed_along(back, "outer", -1)
    return pl.pallas_call(
        functools.partial(finish_kernel, half, groups, members),
        out_shape=(S(queries.shape, BF), S((rows, half), F32), S((rows, half), F32)),
        in_specs=[VMEM] * 4,
        out_specs=(VMEM,) * 3,
        compiler_params=limit(8),
        name="finish",
    )(part, back, own_dq, far_dq)


def solution(mesh):
    tokens = P(("outer", "inner"), None)
    split = P(("outer", "inner"), "dp")
    return jax.shard_map(
        step,
        mesh=mesh,
        in_specs=(split, split, tokens, tokens, P(), P()),
        out_specs=(split, split, split),
        check_vma=False,
    )
```

time: 271 us -> 59 us (0.22)
  the two profiles are of different devices: /device:TPU:32 before, /device:TPU:8 now
where the time goes in v1:
time: 59 us; the launch traced here: 58.5 us
  starting transfers between devices  32.6 us (55%)
  Pallas kernels  13.3 us (23%)
  waiting for transfers between devices  12 us (20%)
  between operations  0.71 us (1%)
    ppermute x4, starting transfers between devices, passed_along(): lax.ppermute(x, axis, [(i, (i + by) % devices) for i in range(devices)])  14.2 us
    all_to_all x1, starting transfers between devices, step(): group_kv = lax.all_to_all(kv4, 'inner', 0, 0, tiled=True)  13.6 us
    ppermute x4, waiting for transfers between devices, passed_along(): lax.ppermute(x, axis, [(i, (i + by) % devices) for i in range(devices)])  12 us
    pallas_call x1, Pallas kernels, step(): pl.pallas_call(functools.partial(heads_kernel, False, half, groups, membe...  5.47 us
    all_to_all x1, starting transfers between devices, step(): part = lax.all_to_all(part, 'inner', 0, 0, tiled=True)  4.8 us
    pallas_call x1, Pallas kernels, step(): pl.pallas_call(functools.partial(heads_kernel, True, half, groups, member...  4.51 us
    pallas_call x1, Pallas kernels, step(): pl.pallas_call(functools.partial(pack_kernel, (groups, half, members, out...  2.31 us
  transfers between devices with their start and end apart: 6, of which 2 were waited for; matrix products, arithmetic and copies ran while one was open for 0% of the time, Pallas kernels for 8%

profile of v1, /device:TPU:8, one launch (start us, length us, event | category | flops | bytes accessed | tf_op | source)
XLA Modules:
  0.0 58.5 jit_solution(2807407060658765115)
XLA Ops:
  0.6 2.3 %pack.1 = (bf16[128,2048]{1,0:T(8,128)(2,1)S(1)}, bf16[512,512]{1,0:T(8,128)(2,1)}, bf16[128,512]{1,0:T(8,128)(2,1)S(1)}, f32[640,128]{1,0:T(8,128)S(1)}) custom-call(s32[512]{0:T(512)} %order_hbm.1, s32[5,512]{1,0:T(8,128)} %bitcast.8, bf16[128,2048]{1,0:T(8,128)(2,1)} %refs_0_.1, bf16[128,2048]{1,0:T(8,128)(2,1)} %refs_1_.1, bf16[128,512]{1,0:T(8,128)(2,1)} %k_ref.1, ...), custom_call_target="tpu_custom_call" | custom-call | tf_op jit(solution)/shard_map/pack/pallas_call | solution.py:192
  2.9 5.0 %collective-permute-start = (bf16[128,2048]{1,0:T(8,128)(2,1)S(1)}, bf16[128,2048]{1,0:T(8,128)(2,1)S(1)}, u32[]{:S(2)}, u32[]{:S(2)}) collective-permute-start(bf16[128,2048]{1,0:T(8,128)(2,1)S(1)} %get-tuple-element.13), channel_id=1, source_target_pairs={{0,512},{512,0},{1,513},{513,1},{2,514},{514,2},{3,515},{515,3},{4... | collective-permute-start | bytes 1572872 | tf_op jit(solution)/shard_map/ppermute | solution.py:24
  8.0 0.0 copy-start
  8.0 0.0 copy-start.1
  8.0 13.6 %all-to-all-start = ((bf16[4,128,512]{2,1,0:T(8,128)(2,1)}), bf16[4,128,512]{2,1,0:T(8,128)(2,1)S(1)}, u32[]{:S(2)}, u32[]{:S(2)}) async-start(bf16[4,128,512]{2,1,0:T(8,128)(2,1)} %bitcast.1), calls=%async_computation | async-start | bytes 1048576 | tf_op jit(solution)/shard_map/all_to_all | solution.py:212
  21.6 1.9 %collective-permute-start.1 = (bf16[128,512]{1,0:T(8,128)(2,1)S(1)}, bf16[128,512]{1,0:T(8,128)(2,1)S(1)}, u32[]{:S(2)}, u32[]{:S(2)}) collective-permute-start(bf16[128,512]{1,0:T(8,128)(2,1)S(1)} %get-tuple-element.15), channel_id=1, source_target_pairs={{0,4},{4,8},{8,12},{12,16},{16,20},{20,24},{24,28},{28,32},{32,36}... | collective-permute-start | bytes 393224 | tf_op jit(solution)/shard_map/ppermute | solution.py:24
  23.5 9.5 %collective-permute-done.1.refs_3_.refs_2_ = bf16[128,512]{1,0:T(8,128)(2,1)S(1)} collective-permute-done((bf16[128,512]{1,0:T(8,128)(2,1)S(1)}, bf16[128,512]{1,0:T(8,128)(2,1)S(1)}, u32[]{:S(2)}, u32[]{:S(2)}) %collective-permute-start.1) | collective-permute-done | bytes 131104 | tf_op jit(solution)/shard_map/ppermute | solution.py:24
  33.0 0.0 all-to-all-done
  33.0 0.0 copy-done
  33.0 0.0 copy-done.1
  33.0 4.5 %own_heads.1 = (bf16[128,1024]{1,0:T(8,128)(2,1)S(1)}, f32[2,640,128]{2,1,0:T(8,128)S(1)}, f32[2,640,128]{2,1,0:T(8,128)S(1)}) custom-call(bf16[128,2048]{1,0:T(8,128)(2,1)S(1)} %copy-done, bf16[128,2048]{1,0:T(8,128)(2,1)S(1)} %copy-done.1, bf16[512,512]{1,0:T(8,128)(2,1)S(1)} %bitcast.6, bf16[128,512]{1,0:T(8,128)(2,1)S(1)} %collective-permute-done.1.refs_3_.refs_2_, ...), custom_call_target="tpu_custom_call" | custom-call | flops 838860800 | bytes 2621440 | tf_op jit(solution)/shard_map/own_heads/pallas_call | solution.py:219
  37.5 0.0 collective-permute-done.refs_0_
  37.5 5.5 %far_heads.1 = (bf16[128,1024]{1,0:T(8,128)(2,1)S(1)}, bf16[512,512]{1,0:T(8,128)(2,1)}, bf16[128,512]{1,0:T(8,128)(2,1)S(1)}) custom-call(bf16[128,2048]{1,0:T(8,128)(2,1)S(1)} %collective-permute-done.refs_0_, bf16[512,512]{1,0:T(8,128)(2,1)S(1)} %bitcast.7, bf16[128,512]{1,0:T(8,128)(2,1)S(1)} %collective-permute-done.1.refs_3_.refs_2_, ...), custom_call_target="tpu_custom_call" | custom-call | flops 838860800 | bytes 2621440 | tf_op jit(solution)/shard_map/far_heads/pallas_call | solution.py:229
  43.0 4.8 %all-to-all-start.1 = ((bf16[4,128,512]{2,1,0:T(8,128)(2,1)}), bf16[4,128,512]{2,1,0:T(8,128)(2,1)S(1)}, u32[]{:S(2)}, u32[]{:S(2)}) async-start(bf16[4,128,512]{2,1,0:T(8,128)(2,1)} %bitcast.3), calls=%async_computation.1 | async-start | bytes 1048576 | tf_op jit(solution)/shard_map/all_to_all | solution.py:240
  47.8 3.8 %collective-permute-start.3 = (bf16[128,1024]{1,0:T(8,128)(2,1)S(1)}, bf16[128,1024]{1,0:T(8,128)(2,1)S(1)}, u32[]{:S(2)}, u32[]{:S(2)}) collective-permute-start(bf16[128,1024]{1,0:T(8,128)(2,1)S(1)} %get-tuple-element.22), channel_id=1, source_target_pairs={{0,512},{512,0},{1,513},{513,1},{2,514},{514,2},{3,515},{515,3},{4... | collective-permute-start | bytes 786440 | tf_op jit(solution)/shard_map/ppermute | solution.py:24
  51.6 3.4 %collective-permute-start.2 = (bf16[128,512]{1,0:T(8,128)(2,1)S(1)}, bf16[128,512]{1,0:T(8,128)(2,1)S(1)}, u32[]{:S(2)}, u32[]{:S(2)}) collective-permute-start(bf16[128,512]{1,0:T(8,128)(2,1)S(1)} %get-tuple-element.20), channel_id=1, source_target_pairs={{0,508},{4,0},{8,4},{12,8},{16,12},{20,16},{24,20},{28,24},{32,28}... | collective-permute-start | bytes 393224 | tf_op jit(solution)/shard_map/ppermute | solution.py:24
  55.1 2.5 %collective-permute-done.2.back_ref = bf16[128,512]{1,0:T(8,128)(2,1)S(1)} collective-permute-done((bf16[128,512]{1,0:T(8,128)(2,1)S(1)}, bf16[128,512]{1,0:T(8,128)(2,1)S(1)}, u32[]{:S(2)}, u32[]{:S(2)}) %collective-permute-start.2) | collective-permute-done | bytes 131104 | tf_op jit(solution)/shard_map/ppermute | solution.py:24
  57.6 0.0 collective-permute-done.3.far_dq_ref
  57.6 0.0 all-to-all-done.1
  57.6 1.0 %finish.1 = (bf16[128,2048]{1,0:T(8,128)(2,1)}, f32[128,256]{1,0:T(8,128)}, f32[128,256]{1,0:T(8,128)}) custom-call(bf16[512,512]{1,0:T(8,128)(2,1)S(1)} %bitcast.5, bf16[128,512]{1,0:T(8,128)(2,1)S(1)} %collective-permute-done.2.back_ref, bf16[128,1024]{1,0:T(8,128)(2,1)S(1)} %get-tuple-element.21.own_dq_ref, ...), custom_call_target="tpu_custom_call" | custom-call | tf_op jit(solution)/shard_map/finish/pallas_call | solution.py:242
Async XLA Ops:
  2.9 34.6 %collective-permute-start = (bf16[128,2048]{1,0:T(8,128)(2,1)S(1)}, bf16[128,2048]{1,0:T(8,128)(2,1)S(1)}, u32[]{:S(2)}, u32[]{:S(2)}) collective-permute-start(bf16[128,2048]{1,0:T(8,128)(2,1)S(1)} %get-tuple-element.13), channel_id=1, source_target_pairs={{0,512},{512,0},{1,513},{513,1},{2,514},{514,2},{3,515},{515,3},{4... | collective-permute-start | bytes 1572872 | tf_op jit(solution)/shard_map/ppermute | solution.py:24
  8.0 25.0 %copy-start = (bf16[128,2048]{1,0:T(8,128)(2,1)S(1)}, bf16[128,2048]{1,0:T(8,128)(2,1)}, u32[]{:S(2)}) copy-start(bf16[128,2048]{1,0:T(8,128)(2,1)} %refs_0_.1) | copy-start | bytes 1572868
  8.0 25.0 %copy-start.1 = (bf16[128,2048]{1,0:T(8,128)(2,1)S(1)}, bf16[128,2048]{1,0:T(8,128)(2,1)}, u32[]{:S(2)}) copy-start(bf16[128,2048]{1,0:T(8,128)(2,1)} %refs_1_.1) | copy-start | bytes 1572868
  8.0 25.0 %all-to-all-start = ((bf16[4,128,512]{2,1,0:T(8,128)(2,1)}), bf16[4,128,512]{2,1,0:T(8,128)(2,1)S(1)}, u32[]{:S(2)}, u32[]{:S(2)}) async-start(bf16[4,128,512]{2,1,0:T(8,128)(2,1)} %bitcast.1), calls=%async_computation | async-start | bytes 1048576 | tf_op jit(solution)/shard_map/all_to_all | solution.py:212
  21.6 11.4 %collective-permute-start.1 = (bf16[128,512]{1,0:T(8,128)(2,1)S(1)}, bf16[128,512]{1,0:T(8,128)(2,1)S(1)}, u32[]{:S(2)}, u32[]{:S(2)}) collective-permute-start(bf16[128,512]{1,0:T(8,128)(2,1)S(1)} %get-tuple-element.15), channel_id=1, source_target_pairs={{0,4},{4,8},{8,12},{12,16},{16,20},{20,24},{24,28},{28,32},{32,36}... | collective-permute-start | bytes 393224 | tf_op jit(solution)/shard_map/ppermute | solution.py:24
  43.0 14.6 %all-to-all-start.1 = ((bf16[4,128,512]{2,1,0:T(8,128)(2,1)}), bf16[4,128,512]{2,1,0:T(8,128)(2,1)S(1)}, u32[]{:S(2)}, u32[]{:S(2)}) async-start(bf16[4,128,512]{2,1,0:T(8,128)(2,1)} %bitcast.3), calls=%async_computation.1 | async-start | bytes 1048576 | tf_op jit(solution)/shard_map/all_to_all | solution.py:240
  47.8 9.8 %collective-permute-start.3 = (bf16[128,1024]{1,0:T(8,128)(2,1)S(1)}, bf16[128,1024]{1,0:T(8,128)(2,1)S(1)}, u32[]{:S(2)}, u32[]{:S(2)}) collective-permute-start(bf16[128,1024]{1,0:T(8,128)(2,1)S(1)} %get-tuple-element.22), channel_id=1, source_target_pairs={{0,512},{512,0},{1,513},{513,1},{2,514},{514,2},{3,515},{515,3},{4... | collective-permute-start | bytes 786440 | tf_op jit(solution)/shard_map/ppermute | solution.py:24
  51.6 5.9 %collective-permute-start.2 = (bf16[128,512]{1,0:T(8,128)(2,1)S(1)}, bf16[128,512]{1,0:T(8,128)(2,1)S(1)}, u32[]{:S(2)}, u32[]{:S(2)}) collective-permute-start(bf16[128,512]{1,0:T(8,128)(2,1)S(1)} %get-tuple-element.20), channel_id=1, source_target_pairs={{0,508},{4,0},{8,4},{12,8},{16,12},{20,16},{24,20},{28,24},{32,28}... | collective-permute-start | bytes 393224 | tf_op jit(solution)/shard_map/ppermute | solution.py:24

commit v2 on v1

--- a/solution.py
+++ b/solution.py
@@ -78,92 +78,115 @@
         copy.wait()
 
 
-def attend(q2, g2, keys, values, keys_t, bias2):
+def attend_kernel(half, groups, members, q_ref, g_ref, qg_ref, kv_ref, prev_ref, bias_ref, own_dq, far_dq, part_ref, back_ref, *scratch):
+    scores, grads, softs, slopes = scratch[0:2], scratch[2:4], scratch[4:6], scratch[6:8]
+    keys_t, key_sum, value_sum = scratch[8:11]
+    rows = prev_ref.shape[0]
+    slots = members + 1
+    per = half // HD
+    wide = groups * half
+    d = lax.axis_index("dp")
     nt = (((1,), (1,)), ((), ()))
-    scores = lax.dot_general(keys, q2, nt, preferred_element_type=F32) + bias2
-    top = jnp.max(scores, axis=0, keepdims=True)
-    exps = jnp.exp2((scores - top) * (SCALE * LOG2E))
-    weight_grads = lax.dot_general(values, g2, nt, preferred_element_type=F32)
-    inverse = 1.0 / jnp.sum(exps, axis=0, keepdims=True)
-    delta = jnp.sum(exps * weight_grads, axis=0, keepdims=True) * inverse
-    soft = exps * inverse
-    soft_low = soft.astype(BF)
-    score_grads = (soft * ((weight_grads - delta) * SCALE)).astype(BF)
-    value_part = jnp.dot(soft_low, g2, preferred_element_type=F32)
-    key_part = jnp.dot(score_grads, q2, preferred_element_type=F32)
-    query_t = jnp.dot(keys_t, score_grads, preferred_element_type=F32)
-    return query_t, key_part, value_part
-
-
-def heads_kernel(local, half, groups, members, *refs):
-    if local:
-        q_ref, g_ref, kv_ref, prev_ref, bias_ref, dq_ref, dk_ref, dv_ref, keys, values, keys_t = refs
-    else:
-        (qg_ref, kv_ref, prev_ref, bias_ref, dk_in, dv_in, dq_ref, part_ref, back_ref, keys, values, keys_t, dk_ref, dv_ref) = refs
-    rows = prev_ref.shape[0]
-    span = members * rows
-    per = half // HD
-    d = lax.axis_index("dp")
+    units = [(j, own, g) for j in range(per) for own in (True, False) for g in range(0, groups, 2)]
+    pack = groups // 2
+
+    def chunk(j, c, base):
+        if c == members:
+            return prev_ref[:, base + j * HD : base + (j + 1) * HD]
+        return kv_ref[c * rows : (c + 1) * rows, base + j * HD : base + (j + 1) * HD]
+
+    def heads(i, grad):
+        j, own, g = units[i]
+        if own:
+            ref = g_ref if grad else q_ref
+            parts = [ref[:, lanes((g + e) * 2 * half + d * half + j * HD, HD)] for e in range(2)]
+        else:
+            base = wide if grad else 0
+            parts = [qg_ref[:, base + (g + e) * half + j * HD : base + (g + e) * half + (j + 1) * HD] for e in range(2)]
+        return jnp.concatenate(parts, 0)
+
+    def fold(x, op):
+        return op(x.reshape(x.shape[0] // 8, 8, x.shape[1]), axis=0)
+
+    def stage_a(i):
+        j = units[i][0]
+        q2, g2 = heads(i, False), heads(i, True)
+        top = None
+        for c in range(slots):
+            at = slice(c * rows, (c + 1) * rows)
+            bias = bias_ref[at, :]
+            s = lax.dot_general(chunk(j, c, 0), q2, nt, preferred_element_type=F32)
+            s = s + jnp.concatenate([bias, bias], 1)
+            scores[i % 2][at, :] = s
+            peak = fold(s, jnp.max)
+            top = peak if top is None else jnp.maximum(top, peak)
+        for c in range(slots):
+            at = slice(c * rows, (c + 1) * rows)
+            grads[i % 2][at, :] = lax.dot_general(chunk(j, c, half), g2, nt, preferred_element_type=F32)
+        return jnp.max(top, axis=0, keepdims=True)
+
+    def stage_b(i, top):
+        total = delta = None
+        for c in range(slots):
+            at = slice(c * rows, (c + 1) * rows)
+            e = jnp.exp2((scores[i % 2][at, :] - top) * (SCALE * LOG2E))
+            scores[i % 2][at, :] = e
+            te, de = fold(e, jnp.sum), fold(e * grads[i % 2][at, :], jnp.sum)
+            total = te if total is None else total + te
+            delta = de if delta is None else delta + de
+        inverse = 1.0 / jnp.sum(total, axis=0, keepdims=True)
+        delta = jnp.sum(delta, axis=0, keepdims=True) * inverse
+        bunch, lane = (i // pack) % 2, (i % pack) * 2 * rows
+        for c in range(slots):
+            at = slice(c * rows, (c + 1) * rows)
+            soft = scores[i % 2][at, :] * inverse
+            softs[bunch][at, lane : lane + 2 * rows] = soft.astype(BF)
+            slope = soft * ((grads[i % 2][at, :] - delta) * SCALE)
+            slopes[bunch][at, lane : lane + 2 * rows] = slope.astype(BF)
+
+    def stage_q(i):
+        j, own, g = units[i]
+        bunch, lane = (i // pack) % 2, (i % pack) * 2 * rows
+        out = jnp.dot(keys_t[j], slopes[bunch][:, lane : lane + 2 * rows], preferred_element_type=F32)
+        ref = own_dq if own else far_dq
+        for e in range(2):
+            at = (g + e) * half + j * HD
+            ref[:, at : at + HD] = out[:, e * rows : (e + 1) * rows].T.astype(BF)
+
+    def stage_kv(k, grad):
+        first = k * pack
+        j, own, _ = units[first]
+        other = jnp.concatenate([heads(first + e, grad) for e in range(pack)], 0)
+        weights, total, base = (softs, value_sum, half) if grad else (slopes, key_sum, 0)
+        for c in range(slots):
+            at = slice(c * rows, (c + 1) * rows)
+            out = jnp.dot(weights[k % 2][at, :], other, preferred_element_type=F32)
+            if own:
+                total[at, :] = out
+                continue
+            out = (total[at, :] + out).astype(BF)
+            lane = slice(base + j * HD, base + (j + 1) * HD)
+            if c == members:
+                back_ref[:, lane] = out
+            else:
+                part_ref[at, lane] = out
+
     for j in range(per):
-        keys[j, :span, :] = kv_ref[:, j * HD : (j + 1) * HD]
-        keys[j, span:, :] = prev_ref[:, j * HD : (j + 1) * HD]
-        values[j, :span, :] = kv_ref[:, half + j * HD : half + (j + 1) * HD]
-        values[j, span:, :] = prev_ref[:, half + j * HD : half + (j + 1) * HD]
-        keys_t[j] = keys[j].T
-    pairs = groups // 2
-
-    def step(i, carry):
-        j, pair = i // pairs, i % pairs
-        wide = groups * half
-        if local:
-            at = [(2 * pair + e) * 2 * half + d * half + j * HD for e in range(2)]
-            q2 = jnp.concatenate([q_ref[:, lanes(a, HD)] for a in at], 0)
-            g2 = jnp.concatenate([g_ref[:, lanes(a, HD)] for a in at], 0)
-        else:
-            at = [(2 * pair + e) * half + j * HD for e in range(2)]
-            q2 = jnp.concatenate([qg_ref[:, lanes(a, HD)] for a in at], 0)
-            g2 = jnp.concatenate([qg_ref[:, lanes(wide + a, HD)] for a in at], 0)
-        bias = bias_ref[...]
-        query_t, key_part, value_part = attend(
-            q2, g2, keys[j], values[j], keys_t[j], jnp.concatenate([bias, bias], 1)
-        )
-        for e in range(2):
-            out_at = (2 * pair + e) * half + j * HD
-            dq_ref[:, lanes(out_at, HD)] = query_t[:, e * rows : (e + 1) * rows].T.astype(BF)
-        if local:
-            first = pair == 0
-
-            @pl.when(first)
-            def _():
-                dk_ref[j] = key_part
-                dv_ref[j] = value_part
-
-            @pl.when(jnp.logical_not(first))
-            def _():
-                dk_ref[j] += key_part
-                dv_ref[j] += value_part
-        else:
-            first = pair == 0
-
-            @pl.when(first)
-            def _():
-                dk_ref[j] = dk_in[j] + key_part
-                dv_ref[j] = dv_in[j] + value_part
-
-            @pl.when(jnp.logical_not(first))
-            def _():
-                dk_ref[j] += key_part
-                dv_ref[j] += value_part
-
-        return carry
-
-    lax.fori_loop(0, per * pairs, step, 0)
-    if not local:
-        for j in range(per):
-            for ref, base in ((dk_ref, 0), (dv_ref, half)):
-                at = base + j * HD
-                part_ref[:, at : at + HD] = ref[j, :span, :].astype(BF)
-                back_ref[:, at : at + HD] = ref[j, span:, :].astype(BF)
+        for c in range(slots):
+            keys_t[j, :, c * rows : (c + 1) * rows] = chunk(j, c, 0).T
+    count = len(units)
+    tops = {}
+    for t in range(count + pack + 2):
+        if t < count:
+            tops[t] = stage_a(t)
+        if 0 <= t - 1 < count:
+            stage_b(t - 1, tops.pop(t - 1))
+        if 0 <= t - 2 < count:
+            stage_q(t - 2)
+        for lag, grad in ((pack, True), (pack + 1, False)):
+            k, rest = divmod(t - lag - 1, pack)
+            if rest == 0 and 0 <= k < count // pack:
+                stage_kv(k, grad)
 
 
 def finish_kernel(half, groups, members, part_ref, back_ref, own_dq_ref, far_dq_ref, dq_ref, dk_ref, dv_ref):
@@ -210,32 +233,28 @@
     prev_kv = passed_along(kv, "outer", 1)
     received = passed_along(send, "dp", 1)
     group_kv = lax.all_to_all(kv4, "inner", 0, 0, tiled=True)
-    scratch = [pltpu.VMEM((per, window, HD), BF), pltpu.VMEM((per, window, HD), BF), pltpu.VMEM((per, HD, window), BF)]
     cost = pl.CostEstimate(
-        flops=10 * rows * window * HD * groups * per,
-        transcendentals=rows * window * groups * per,
-        bytes_accessed=4 * rows * window * per * groups,
+        flops=20 * rows * window * HD * groups * per,
+        transcendentals=2 * rows * window * groups * per,
+        bytes_accessed=8 * rows * window * per * groups,
     )
-    own_dq, dk, dv = pl.pallas_call(
-        functools.partial(heads_kernel, True, half, groups, members),
-        out_shape=(S((rows, groups * half), BF), S((per, window, HD), F32), S((per, window, HD), F32)),
-        in_specs=[VMEM] * 5,
-        out_specs=(VMEM,) * 3,
-        scratch_shapes=scratch,
+    own_dq, far_dq, part, back = pl.pallas_call(
+        functools.partial(attend_kernel, half, groups, members),
+        out_shape=(
+            S((rows, groups * half), BF),
+            S((rows, groups * half), BF),
+            S((members * rows, 2 * half), BF),
+            S((rows, 2 * half), BF),
+        ),
+        in_specs=[VMEM] * 6,
+        out_specs=(VMEM,) * 4,
+        scratch_shapes=[pltpu.VMEM((window, 2 * rows), F32)] * 4
+        + [pltpu.VMEM((window, groups * rows), BF)] * 4
+        + [pltpu.VMEM((per, HD, window), BF), pltpu.VMEM((window, HD), F32), pltpu.VMEM((window, HD), F32)],
         cost_estimate=cost,
         compiler_params=limit(24),
-        name="own_heads",
-    )(queries, out_grad, group_kv, prev_kv, bias)
-    far_dq, part, back = pl.pallas_call(
-        functools.partial(heads_kernel, False, half, groups, members),
-        out_shape=(S((rows, groups * half), BF), S((members * rows, 2 * half), BF), S((rows, 2 * half), BF)),
-        in_specs=[VMEM] * 6,
-        out_specs=(VMEM,) * 3,
-        scratch_shapes=scratch + [pltpu.VMEM((per, window, HD), F32), pltpu.VMEM((per, window, HD), F32)],
-        cost_estimate=cost,
-        compiler_params=limit(24),
-        name="far_heads",
-    )(received, group_kv, prev_kv, bias, dk, dv)
+        name="attend",
+    )(queries, out_grad, received, group_kv, prev_kv, bias)
     far_dq = passed_along(far_dq, "dp", 1)
     part = lax.all_to_all(part, "inner", 0, 0, tiled=True)
     back = passed_along(back, "outer", -1)

time: 59 us -> 57.6 us (0.976)
  Pallas kernels: 13.3 us -> 9.14 us
  starting transfers between devices: 32.6 us -> 35.3 us
    pallas_call x2 -> x1, Pallas kernels: 9.98 us -> 5.87 us  [step(): pl.pallas_call(functools.partial(attend_kernel, half, groups, members), o...]
    ppermute x4, starting transfers between devices: 14.2 us -> 16.9 us  [passed_along(): lax.ppermute(x, axis, [(i, (i + by) % devices) for i in range(devices)])]
  transfers between devices with their start and end apart: 6 -> 6, of which waited for: 2 -> 2; matrix products, arithmetic and copies ran while one was open for 0% -> 0% of each run, Pallas kernels for 8% -> 0%
where the time goes in v2:
time: 57.6 us; the launch traced here: 57.2 us
  starting transfers between devices  35.3 us (61%)
  waiting for transfers between devices  12 us (21%)
  Pallas kernels  9.14 us (16%)
  between operations  0.7 us (1%)
    ppermute x4, starting transfers between devices, passed_along(): lax.ppermute(x, axis, [(i, (i + by) % devices) for i in range(devices)])  16.9 us
    all_to_all x1, starting transfers between devices, step(): group_kv = lax.all_to_all(kv4, 'inner', 0, 0, tiled=True)  13.6 us
    ppermute x4, waiting for transfers between devices, passed_along(): lax.ppermute(x, axis, [(i, (i + by) % devices) for i in range(devices)])  12 us
    pallas_call x1, Pallas kernels, step(): pl.pallas_call(functools.partial(attend_kernel, half, groups, members), o...  5.87 us
    all_to_all x1, starting transfers between devices, step(): part = lax.all_to_all(part, 'inner', 0, 0, tiled=True)  4.8 us
    pallas_call x1, Pallas kernels, step(): pl.pallas_call(functools.partial(pack_kernel, (groups, half, members, out...  2.31 us
  transfers between devices with their start and end apart: 6, of which 2 were waited for; matrix products, arithmetic and copies ran while one was open for 0% of the time, Pallas kernels for 0%

profile of v2, /device:TPU:8, one launch (start us, length us, event | category | flops | bytes accessed | tf_op | source)
XLA Modules:
  0.0 57.2 jit_solution(751042656631826745)
XLA Ops:
  0.6 2.3 %pack.1 = (bf16[128,2048]{1,0:T(8,128)(2,1)S(1)}, bf16[512,512]{1,0:T(8,128)(2,1)}, bf16[128,512]{1,0:T(8,128)(2,1)S(1)}, f32[640,128]{1,0:T(8,128)S(1)}) custom-call(s32[512]{0:T(512)} %order_hbm.1, s32[5,512]{1,0:T(8,128)} %bitcast.7, bf16[128,2048]{1,0:T(8,128)(2,1)} %q_ref.3, bf16[128,2048]{1,0:T(8,128)(2,1)} %g_ref.3, bf16[128,512]{1,0:T(8,128)(2,1)} %k_ref.1, ...), custom_call_target="tpu_custom_call" | custom-call | tf_op jit(solution)/shard_map/pack/pallas_call | solution.py:215
  2.9 5.0 %collective-permute-start = (bf16[128,2048]{1,0:T(8,128)(2,1)S(1)}, bf16[128,2048]{1,0:T(8,128)(2,1)S(1)}, u32[]{:S(2)}, u32[]{:S(2)}) collective-permute-start(bf16[128,2048]{1,0:T(8,128)(2,1)S(1)} %get-tuple-element.11), channel_id=1, source_target_pairs={{0,512},{512,0},{1,513},{513,1},{2,514},{514,2},{3,515},{515,3},{4... | collective-permute-start | bytes 1572872 | tf_op jit(solution)/shard_map/ppermute | solution.py:24
  8.0 0.0 copy-start
  8.0 0.0 copy-start.1
  8.0 13.6 %all-to-all-start = ((bf16[4,128,512]{2,1,0:T(8,128)(2,1)}), bf16[4,128,512]{2,1,0:T(8,128)(2,1)S(1)}, u32[]{:S(2)}, u32[]{:S(2)}) async-start(bf16[4,128,512]{2,1,0:T(8,128)(2,1)} %bitcast.1), calls=%async_computation | async-start | bytes 1048576 | tf_op jit(solution)/shard_map/all_to_all | solution.py:235
  21.6 1.9 %collective-permute-start.1 = (bf16[128,512]{1,0:T(8,128)(2,1)S(1)}, bf16[128,512]{1,0:T(8,128)(2,1)S(1)}, u32[]{:S(2)}, u32[]{:S(2)}) collective-permute-start(bf16[128,512]{1,0:T(8,128)(2,1)S(1)} %get-tuple-element.13), channel_id=1, source_target_pairs={{0,4},{4,8},{8,12},{12,16},{16,20},{20,24},{24,28},{28,32},{32,36}... | collective-permute-start | bytes 393224 | tf_op jit(solution)/shard_map/ppermute | solution.py:24
  23.5 9.5 %collective-permute-done.1.prev_ref = bf16[128,512]{1,0:T(8,128)(2,1)S(1)} collective-permute-done((bf16[128,512]{1,0:T(8,128)(2,1)S(1)}, bf16[128,512]{1,0:T(8,128)(2,1)S(1)}, u32[]{:S(2)}, u32[]{:S(2)}) %collective-permute-start.1) | collective-permute-done | bytes 131104 | tf_op jit(solution)/shard_map/ppermute | solution.py:24
  33.0 0.0 all-to-all-done
  33.0 0.0 collective-permute-done.qg_ref
  33.0 0.0 copy-done
  33.0 0.0 copy-done.1
  33.0 5.9 %attend.1 = (bf16[128,1024]{1,0:T(8,128)(2,1)S(1)}, bf16[128,1024]{1,0:T(8,128)(2,1)S(1)}, bf16[512,512]{1,0:T(8,128)(2,1)}, bf16[128,512]{1,0:T(8,128)(2,1)S(1)}) custom-call(bf16[128,2048]{1,0:T(8,128)(2,1)S(1)} %copy-done, bf16[128,2048]{1,0:T(8,128)(2,1)S(1)} %copy-done.1, bf16[128,2048]{1,0:T(8,128)(2,1)S(1)} %collective-permute-done.qg_ref, ...), custom_call_target="tpu_custom_call" | custom-call | flops 1677721600 | bytes 5242880 | tf_op jit(solution)/shard_map/attend/pallas_call | solution.py:241
  38.9 4.8 %all-to-all-start.1 = ((bf16[4,128,512]{2,1,0:T(8,128)(2,1)}), bf16[4,128,512]{2,1,0:T(8,128)(2,1)S(1)}, u32[]{:S(2)}, u32[]{:S(2)}) async-start(bf16[4,128,512]{2,1,0:T(8,128)(2,1)} %bitcast.3), calls=%async_computation.1 | async-start | bytes 1048576 | tf_op jit(solution)/shard_map/all_to_all | solution.py:259
  43.7 3.9 %collective-permute-start.3 = (bf16[128,1024]{1,0:T(8,128)(2,1)S(1)}, bf16[128,1024]{1,0:T(8,128)(2,1)S(1)}, u32[]{:S(2)}, u32[]{:S(2)}) collective-permute-start(bf16[128,1024]{1,0:T(8,128)(2,1)S(1)} %get-tuple-element.18), channel_id=1, source_target_pairs={{0,512},{512,0},{1,513},{513,1},{2,514},{514,2},{3,515},{515,3},{4... | collective-permute-start | bytes 786440 | tf_op jit(solution)/shard_map/ppermute | solution.py:24
  47.6 6.1 %collective-permute-start.2 = (bf16[128,512]{1,0:T(8,128)(2,1)S(1)}, bf16[128,512]{1,0:T(8,128)(2,1)S(1)}, u32[]{:S(2)}, u32[]{:S(2)}) collective-permute-start(bf16[128,512]{1,0:T(8,128)(2,1)S(1)} %get-tuple-element.16), channel_id=1, source_target_pairs={{0,508},{4,0},{8,4},{12,8},{16,12},{20,16},{24,20},{28,24},{32,28}... | collective-permute-start | bytes 393224 | tf_op jit(solution)/shard_map/ppermute | solution.py:24
  53.7 2.5 %collective-permute-done.2.back_ref = bf16[128,512]{1,0:T(8,128)(2,1)S(1)} collective-permute-done((bf16[128,512]{1,0:T(8,128)(2,1)S(1)}, bf16[128,512]{1,0:T(8,128)(2,1)S(1)}, u32[]{:S(2)}, u32[]{:S(2)}) %collective-permute-start.2) | collective-permute-done | bytes 131104 | tf_op jit(solution)/shard_map/ppermute | solution.py:24
  56.2 0.0 collective-permute-done.3.far_dq_ref
  56.2 0.0 all-to-all-done.1
  56.2 1.0 %finish.1 = (bf16[128,2048]{1,0:T(8,128)(2,1)}, f32[128,256]{1,0:T(8,128)}, f32[128,256]{1,0:T(8,128)}) custom-call(bf16[512,512]{1,0:T(8,128)(2,1)S(1)} %bitcast.5, bf16[128,512]{1,0:T(8,128)(2,1)S(1)} %collective-permute-done.2.back_ref, bf16[128,1024]{1,0:T(8,128)(2,1)S(1)} %get-tuple-element.17.own_dq_ref, ...), custom_call_target="tpu_custom_call" | custom-call | tf_op jit(solution)/shard_map/finish/pallas_call | solution.py:261
Async XLA Ops:
  2.9 30.0 %collective-permute-start = (bf16[128,2048]{1,0:T(8,128)(2,1)S(1)}, bf16[128,2048]{1,0:T(8,128)(2,1)S(1)}, u32[]{:S(2)}, u32[]{:S(2)}) collective-permute-start(bf16[128,2048]{1,0:T(8,128)(2,1)S(1)} %get-tuple-element.11), channel_id=1, source_target_pairs={{0,512},{512,0},{1,513},{513,1},{2,514},{514,2},{3,515},{515,3},{4... | collective-permute-start | bytes 1572872 | tf_op jit(solution)/shard_map/ppermute | solution.py:24
  8.0 25.0 %copy-start = (bf16[128,2048]{1,0:T(8,128)(2,1)S(1)}, bf16[128,2048]{1,0:T(8,128)(2,1)}, u32[]{:S(2)}) copy-start(bf16[128,2048]{1,0:T(8,128)(2,1)} %q_ref.3) | copy-start | bytes 1572868
  8.0 25.0 %copy-start.1 = (bf16[128,2048]{1,0:T(8,128)(2,1)S(1)}, bf16[128,2048]{1,0:T(8,128)(2,1)}, u32[]{:S(2)}) copy-start(bf16[128,2048]{1,0:T(8,128)(2,1)} %g_ref.3) | copy-start | bytes 1572868
  8.0 25.0 %all-to-all-start = ((bf16[4,128,512]{2,1,0:T(8,128)(2,1)}), bf16[4,128,512]{2,1,0:T(8,128)(2,1)S(1)}, u32[]{:S(2)}, u32[]{:S(2)}) async-start(bf16[4,128,512]{2,1,0:T(8,128)(2,1)} %bitcast.1), calls=%async_computation | async-start | bytes 1048576 | tf_op jit(solution)/shard_map/all_to_all | solution.py:235
  21.6 11.4 %collective-permute-start.1 = (bf16[128,512]{1,0:T(8,128)(2,1)S(1)}, bf16[128,512]{1,0:T(8,128)(2,1)S(1)}, u32[]{:S(2)}, u32[]{:S(2)}) collective-permute-start(bf16[128,512]{1,0:T(8,128)(2,1)S(1)} %get-tuple-element.13), channel_id=1, source_target_pairs={{0,4},{4,8},{8,12},{12,16},{16,20},{20,24},{24,28},{28,32},{32,36}... | collective-permute-start | bytes 393224 | tf_op jit(solution)/shard_map/ppermute | solution.py:24
  38.9 17.3 %all-to-all-start.1 = ((bf16[4,128,512]{2,1,0:T(8,128)(2,1)}), bf16[4,128,512]{2,1,0:T(8,128)(2,1)S(1)}, u32[]{:S(2)}, u32[]{:S(2)}) async-start(bf16[4,128,512]{2,1,0:T(8,128)(2,1)} %bitcast.3), calls=%async_computation.1 | async-start | bytes 1048576 | tf_op jit(solution)/shard_map/all_to_all | solution.py:259
  43.7 12.5 %collective-permute-start.3 = (bf16[128,1024]{1,0:T(8,128)(2,1)S(1)}, bf16[128,1024]{1,0:T(8,128)(2,1)S(1)}, u32[]{:S(2)}, u32[]{:S(2)}) collective-permute-start(bf16[128,1024]{1,0:T(8,128)(2,1)S(1)} %get-tuple-element.18), channel_id=1, source_target_pairs={{0,512},{512,0},{1,513},{513,1},{2,514},{514,2},{3,515},{515,3},{4... | collective-permute-start | bytes 786440 | tf_op jit(solution)/shard_map/ppermute | solution.py:24
  47.6 8.6 %collective-permute-start.2 = (bf16[128,512]{1,0:T(8,128)(2,1)S(1)}, bf16[128,512]{1,0:T(8,128)(2,1)S(1)}, u32[]{:S(2)}, u32[]{:S(2)}) collective-permute-start(bf16[128,512]{1,0:T(8,128)(2,1)S(1)} %get-tuple-element.16), channel_id=1, source_target_pairs={{0,508},{4,0},{8,4},{12,8},{16,12},{20,16},{24,20},{28,24},{32,28}... | collective-permute-start | bytes 393224 | tf_op jit(solution)/shard_map/ppermute | solution.py:24
